TPU v7x, 128 devices: a whole 4x4x4 slice. The times are simulated.
128 devices in a mesh: grp: 4 (over x_hi, core), vec: 32 (over z, y, x_lo).
Axes of the slice: x: 4 (x_hi: 2, x_lo: 2; x = x_hi * 2 + x_lo), y: 4, z: 4, core: 2. Of those that a mesh axis runs over, the one named last changes fastest.
Arguments:
- vv_vectors: bfloat16 [1280, 1000, 1000], P(('grp', 'vec')), may hold values from -0.1875 to 0.1875
- oo_vectors: bfloat16 [1280, 100, 100], P(('grp', 'vec')), may hold values from -0.625 to 0.625
- ov_slab: bfloat16 [1280, 1024], P(('grp', 'vec')), may hold values from -0.15625 to 0.15625
- amplitudes: bfloat16 [100, 1000], P('grp'), may hold values from -6 to 6
Outputs:
- sigma_slab: float32 [96000, 1024], P(('grp', 'vec'))
All inputs are finite; a program needn't handle non-finite values.
Results may differ from a plain program's by a relative error of at most 0.0029.
Values may be sent and summed in bfloat16 or wider, within the bound.
No kernel may reach another device: no remote copies, remote signals or barrier semaphores. Data moves between devices by JAX's collectives and lax.ppermute only.
A program may use at most 128 MiB of HBM per device.

v0:
```python
import jax
import jax.numpy as jnp
from jax import lax
from jax.sharding import PartitionSpec as P

NV = 1000
I_ROWS = 96


def laid_out(blocks, dim):
    dims = list(blocks.shape[1:])
    dims[dim] *= blocks.shape[0]
    return jnp.moveaxis(blocks, 0, dim).reshape(dims)


def from_everyone(array, axis):
    size = lax.axis_size(axis)
    return lax.all_to_all(
        jnp.broadcast_to(array[None], (size, *array.shape)), axis, 0, 0, tiled=True
    )


def collect(array, axis, dim):
    return laid_out(from_everyone(array, axis), dim)


def split_up(array, dim, size):
    dims = array.shape
    blocks = array.reshape(*dims[:dim], size, dims[dim] // size, *dims[dim + 1 :])
    return jnp.moveaxis(blocks, dim, 0)


def joined_exchange(array, axis, axes, splits, concats):
    sizes = [lax.axis_size(a) for a in axes]
    blocks = split_up(array, splits[0], sizes[0])
    blocks = jnp.moveaxis(split_up(blocks, splits[1] + 1, sizes[1]), 0, 1)
    inside = blocks.shape[2:]
    blocks = blocks.reshape(-1, *inside)
    blocks = lax.all_to_all(blocks, axis, split_axis=0, concat_axis=0, tiled=True)
    blocks = laid_out(blocks.reshape(*sizes, *inside), concats[0] + 1)
    return laid_out(blocks, concats[1])


def shards(vv_vectors, oo_vectors, ov_slab, amplitudes):
    amps_all = collect(amplitudes, "grp", 0)
    window = amps_all[:I_ROWS]
    local_count = vv_vectors.shape[0]
    direct_term = jnp.einsum("ib,pab->pia", window, vv_vectors, preferred_element_type=jnp.float32)
    hole_term = jnp.einsum(
        "pji,ja->pia", oo_vectors[:, :, :I_ROWS], amps_all, preferred_element_type=jnp.float32
    )
    dressed = (direct_term - hole_term).astype(jnp.bfloat16).reshape(local_count, I_ROWS * NV)
    regrouped = joined_exchange(dressed, ("grp", "vec"), ("grp", "vec"), (1, 1), (0, 0))
    group_slab = collect(ov_slab, "grp", 0)
    return lax.dot_general(
        regrouped,
        lax.all_gather(group_slab, "vec", axis=0, tiled=True),
        (((0,), (0,)), ((), ())),
        preferred_element_type=jnp.float32,
    )


def solution(mesh):
    return jax.shard_map(
        shards,
        mesh=mesh,
        in_specs=(
            P(("grp", "vec"), None, None),
            P(("grp", "vec"), None, None),
            P(("grp", "vec"), None),
            P("grp", None),
        ),
        out_specs=P(("grp", "vec"), None),
        check_vma=False,
    )
```

profile of v0, /device:TPU:4, one launch (start us, length us, event | category | flops | bytes accessed | tf_op | source)
XLA Modules:
  0.0 197.3 jit_solution(13646007314827454208)
XLA Ops:
  6.5 0.0 all-gather.2.cloned.1.call-start
  6.5 0.8 broadcast_in_dim.5
  7.3 7.6 %all_to_all.15 = bf16[4,10,1024]{2,1,0:T(8,128)(2,1)S(1)} all-to-all(bf16[4,10,1024]{2,1,0:T(8,128)(2,1)S(1)} %broadcast_in_dim.5), channel_id=1, replica_groups=mesh['grp'=4,'vec'=32] {'grp'}, dimensions={0} | all-to-all | bytes 163840 | tf_op jit(solution)/shard_map/all_to_all | solution.py:18
  14.9 0.7 reshape.21
  15.5 0.0 all-gather.2.cloned.1.call-update
  15.6 0.9 broadcast_in_dim.4
  16.4 9.9 %all_to_all.16 = bf16[4,25,1000]{2,1,0:T(8,128)(2,1)S(1)} all-to-all(bf16[4,25,1000]{2,1,0:T(8,128)(2,1)S(1)} %broadcast_in_dim.4), channel_id=1, replica_groups=mesh['grp'=4,'vec'=32] {'grp'}, dimensions={0} | all-to-all | bytes 400000 | tf_op jit(solution)/shard_map/all_to_all | solution.py:18
  26.3 0.1 reshape.17
  26.4 0.1 reshape.23
  26.5 0.0 copy-start
  26.5 10.3 %fusion.2 = f32[10,1000,96]{1,2,0:T(8,128)S(1)} fusion(bf16[10,1000,1000]{2,1,0:T(8,128)(2,1)} %param.4, bf16[100,1000]{1,0:T(8,128)(2,1)S(1)} %reshape.17), kind=kOutput, calls=%fused_computation.4 | convolution fusion | flops 1920000000 | bytes 24036608 | tf_op jit(solution)/shard_map/ib,pab->pia/dot_general | solution.py:48
  36.8 0.0 copy-done
  36.8 0.7 fusion
  37.6 4.3 %reshape_reshape.6 = bf16[10,4,24000]{2,1,0:T(4,128)(2,1)} reshape(bf16[10,96,1000]{2,1,0:T(8,128)(2,1)S(1)} %fusion) | data formatting | bytes 3840000 | tf_op jit(solution)/shard_map/reshape;reshape | solution.py:29
  41.9 6.0 %reshape.18 = bf16[4,10,32,750]{3,2,0,1:T(8,128)(2,1)S(1)} reshape(bf16[4,10,24000]{2,0,1:T(4,128)(2,1)} %bitcast.22) | data formatting | bytes 3840000 | tf_op jit(solution)/shard_map/reshape | solution.py:29
  47.9 1.2 copy.10
  49.1 70.7 %all_to_all.17 = bf16[128,10,750]{2,1,0:T(8,128)(2,1)S(1)} all-to-all(bf16[128,10,750]{2,1,0:T(8,128)(2,1)S(1)} %bitcast.20), channel_id=1, replica_groups=mesh['grp'=4,'vec'=32] {'grp','vec'}, dimensions={0} | all-to-all | bytes 3840000 | tf_op jit(solution)/shard_map/all_to_all | solution.py:39
  119.8 0.4 copy.12
  120.2 2.5 %reshape_reshape.7 = bf16[1280,750]{1,0:T(8,128)(2,1)} reshape(bf16[32,4,10,750]{3,2,1,0:T(8,128)(2,1)S(1)} %copy.12) | data formatting | bytes 3840000 | tf_op jit(solution)/shard_map/reshape;reshape | solution.py:13
  122.7 61.6 %all-gather.2.cloned.1.call-done = bf16[1280,1024]{1,0:T(8,128)(2,1)} async-done(((bf16[40,1024]{1,0:T(8,128)(2,1)}), bf16[1280,1024]{1,0:T(8,128)(2,1)}) %all-gather.2.cloned.1.call-update) | async-done | bytes 2621456 | tf_op jit(solution)/shard_map/all_gather | solution.py:57
  184.3 6.2 %fusion.3 = f32[750,1024]{1,0:T(8,128)} fusion(bf16[1280,750]{1,0:T(8,128)(2,1)} %reshape_reshape.7, bf16[1280,1024]{1,0:T(8,128)(2,1)} %all-gather.2.cloned.1.call-done), kind=kOutput, calls=%fused_computation.5 | convolution fusion | flops 1966080000 | bytes 7613440 | tf_op jit(solution)/shard_map/dot_general | solution.py:55
Async XLA Ops:
  6.5 177.8 %all-gather.2.cloned.1.call-start = ((), (), s32[]{:S(2)}) async-start(), calls=%async_computation.3 | async-start | bytes 2703360 | tf_op jit(solution)/shard_map/all_gather | solution.py:57
  26.5 10.3 %copy-start = (bf16[10,100,100]{2,1,0:T(8,128)(2,1)S(1)}, bf16[10,100,100]{2,1,0:T(8,128)(2,1)}, u32[]{:S(2)}) copy-start(bf16[10,100,100]{2,1,0:T(8,128)(2,1)} %param.5) | copy-start | bytes 600004
Sparse Core Ops, SparseCore 0:
  15.7 168.5 all-gather.1
where the time goes:
time: 198 us; the launch traced here: 197 us
  blocking collectives  88.1 us (44%)
  waiting for transfers between devices  61.6 us (31%)
  matrix products  17.2 us (9%)
  local copies, waits for them, and re-layouts  16.9 us (9%)
  between operations  13.5 us (7%)
    all_to_all x1, blocking collectives, joined_exchange(): lax.all_to_all(blocks, axis, split_axis=0, concat_axis=0, tiled=True)  70.7 us
    all_gather x1, waiting for transfers between devices, shards(): lax.all_gather(group_slab, 'vec', axis=0, tiled=True)  61.6 us
    all_to_all x2, blocking collectives, from_everyone(): lax.all_to_all(jnp.broadcast_to(array[None], (size, *array.shape)), axis,...  17.5 us
    dot_general x1, matrix products, shards(): jnp.einsum('ib,pab->pia', window, vv_vectors, preferred_element_type=jnp....  10.3 us
    reshape x2, local copies, waits for them, and re-layouts, split_up(): array.reshape(*dims[:dim], size, dims[dim] // size, *dims[dim + 1:])  7.22 us
    dot_general x1, matrix products, shards(): lax.dot_general(regrouped, lax.all_gather(group_slab, 'vec', axis=0, tile...  6.16 us
    another operation x1, local copies, waits for them, and re-layouts, split_up(): array.reshape(*dims[:dim], size, dims[dim] // size, *dims[dim + 1:])  4.33 us
  transfers between devices with their start and end apart: 1, of which 1 were waited for; matrix products, arithmetic and copies ran while one was open for 13% of the time, Pallas kernels for 0%

commit v1 on v0

--- a/solution.py
+++ b/solution.py
@@ -5,6 +5,11 @@
 
 NV = 1000
 I_ROWS = 96
+
+
+def gather_over(block, name, dim):
+    stack = jnp.stack([block] * lax.axis_size(name))
+    return jnp.concatenate(lax.all_to_all(stack, name, 0, 0), axis=dim)
 
 
 def laid_out(blocks, dim):
@@ -54,7 +59,7 @@
     group_slab = collect(ov_slab, "grp", 0)
     return lax.dot_general(
         regrouped,
-        lax.all_gather(group_slab, "vec", axis=0, tiled=True),
+        gather_over(group_slab, "vec", 0),
         (((0,), (0,)), ((), ())),
         preferred_element_type=jnp.float32,
     )

time: 198 us -> 148 us (0.75)
  blocking collectives: 88.1 us -> 8.97 us
  starting transfers between devices: 0.01 us -> 21.7 us
  between operations: 13.5 us -> 0.08 us
  waiting for transfers between devices: 61.6 us -> 71.4 us
  local copies, waits for them, and re-layouts: 16.9 us -> 23.5 us
  matrix products: 17.2 us -> 20.8 us
    all_to_all x0 -> x3, waiting for transfers between devices: none -> 71.4 us  [the longest x1 40.6 us: joined_exchange(): lax.all_to_all(blocks, axis, split_axis=0, concat_axis=0, tiled=True)]
    all_to_all x1 -> x0, blocking collectives: 70.7 us -> none  [joined_exchange(): lax.all_to_all(blocks, axis, split_axis=0, concat_axis=0, tiled=True)]
    all_gather x1 -> x0, waiting for transfers between devices: 61.6 us -> none  [shards(): lax.all_gather(group_slab, 'vec', axis=0, tiled=True)]
    all_to_all x0 -> x3, starting transfers between devices: none -> 21.7 us  [the longest x1 10.5 us: joined_exchange(): lax.all_to_all(blocks, axis, split_axis=0, concat_axis=0, tiled=True)]
    all_to_all x2 -> x1, blocking collectives: 17.5 us -> 8.97 us  [from_everyone(): lax.all_to_all(jnp.broadcast_to(array[None], (size, *array.shape)), axis,...]
    dot_general x1, matrix products: 0.72 us -> 2.83 us  [shards(): jnp.einsum('pji,ja->pia', oo_vectors[:, :, :I_ROWS], amps_all, preferred_...]
    dot_general x1, matrix products: 10.3 us -> 12.4 us  [shards(): jnp.einsum('ib,pab->pia', window, vv_vectors, preferred_element_type=jnp....]
  transfers between devices with their start and end apart: 1 -> 3, of which waited for: 1 -> 2; matrix products, arithmetic and copies ran while one was open for 13% -> 24% of each run, Pallas kernels for 0% -> 0%
where the time goes in v1:
time: 148 us; the launch traced here: 146 us
  waiting for transfers between devices  71.4 us (48%)
  local copies, waits for them, and re-layouts  23.5 us (16%)
  starting transfers between devices  21.7 us (15%)
  matrix products  20.8 us (14%)
  blocking collectives  8.97 us (6%)
    all_to_all x1, waiting for transfers between devices, joined_exchange(): lax.all_to_all(blocks, axis, split_axis=0, concat_axis=0, tiled=True)  40.6 us
    all_to_all x1, waiting for transfers between devices, gather_over(): return jnp.concatenate(lax.all_to_all(stack, name, 0, 0), axis=dim)  30.8 us
    dot_general x1, matrix products, shards(): jnp.einsum('ib,pab->pia', window, vv_vectors, preferred_element_type=jnp....  12.4 us
    all_to_all x1, starting transfers between devices, joined_exchange(): lax.all_to_all(blocks, axis, split_axis=0, concat_axis=0, tiled=True)  10.5 us
    all_to_all x1, blocking collectives, from_everyone(): lax.all_to_all(jnp.broadcast_to(array[None], (size, *array.shape)), axis,...  8.97 us
    reshape x2, local copies, waits for them, and re-layouts, split_up(): array.reshape(*dims[:dim], size, dims[dim] // size, *dims[dim + 1:])  8.87 us
    all_to_all x1, starting transfers between devices, from_everyone(): lax.all_to_all(jnp.broadcast_to(array[None], (size, *array.shape)), axis,...  6.43 us
    dot_general x1, matrix products, shards(): lax.dot_general(regrouped, gather_over(group_slab, 'vec', 0), (((0,), (0,...  5.57 us
  transfers between devices with their start and end apart: 3, of which 2 were waited for; matrix products, arithmetic and copies ran while one was open for 24% of the time, Pallas kernels for 0%

profile of v1, /device:TPU:4, one launch (start us, length us, event | category | flops | bytes accessed | tf_op | source)
XLA Modules:
  0.0 146.5 jit_solution(1865740219389505840)
XLA Ops:
  0.0 0.9 broadcast_in_dim.4
  0.9 9.0 %all_to_all.20 = bf16[4,25,1000]{2,1,0:T(8,128)(2,1)S(1)} all-to-all(bf16[4,25,1000]{2,1,0:T(8,128)(2,1)S(1)} %broadcast_in_dim.4), channel_id=1, replica_groups=mesh['grp'=4,'vec'=32] {'grp'}, dimensions={0} | all-to-all | bytes 400000 | tf_op jit(solution)/shard_map/all_to_all | solution.py:23
  9.8 1.4 broadcast_in_dim.5
  11.3 6.4 %all-to-all-start.2 = ((bf16[4,10,1024]{2,1,0:T(8,128)(2,1)}), bf16[4,10,1024]{2,1,0:T(8,128)(2,1)S(1)}, u32[]{:S(2)}, u32[]{:S(2)}) async-start(bf16[4,10,1024]{2,1,0:T(8,128)(2,1)} %broadcast_in_dim.5), calls=%async_computation.2 | async-start | bytes 262144 | tf_op jit(solution)/shard_map/all_to_all | solution.py:23
  17.7 0.1 reshape.19
  17.8 0.0 copy-start
  17.8 12.4 %fusion.2 = f32[10,1000,96]{1,2,0:T(8,128)} fusion(bf16[10,1000,1000]{2,1,0:T(8,128)(2,1)} %param.4, bf16[100,1000]{1,0:T(8,128)(2,1)S(1)} %reshape.19), kind=kOutput, calls=%fused_computation.4 | convolution fusion | flops 1920000000 | bytes 24036608 | tf_op jit(solution)/shard_map/ib,pab->pia/dot_general | solution.py:53
  30.2 0.1 reshape.25
  30.2 0.0 copy-done
  30.3 2.8 %fusion = bf16[10,96,1000]{2,1,0:T(8,128)(2,1)S(1)} fusion(f32[10,1000,96]{1,2,0:T(8,128)} %fusion.2, bf16[100,1000,1]{1,0,2:T(8,128)(2,1)S(1)} %reshape.25, bf16[10,100,100]{2,1,0:T(8,128)(2,1)S(1)} %copy-done), kind=kOutput, calls=%fused_computation.1 | convolution fusion | flops 193920000 | bytes 6160000 | tf_op jit(solution)/shard_map/pji,ja->pia/dot_general | solution.py:54
  33.1 4.3 %reshape_reshape.6 = bf16[10,4,24000]{2,1,0:T(4,128)(2,1)} reshape(bf16[10,96,1000]{2,1,0:T(8,128)(2,1)S(1)} %fusion) | data formatting | bytes 3840000 | tf_op jit(solution)/shard_map/reshape;reshape | solution.py:34
  37.4 6.0 %reshape.20 = bf16[4,10,32,750]{3,2,0,1:T(8,128)(2,1)S(1)} reshape(bf16[4,10,24000]{2,0,1:T(4,128)(2,1)} %bitcast.23) | data formatting | bytes 3840000 | tf_op jit(solution)/shard_map/reshape | solution.py:34
  43.5 2.8 %copy.10 = bf16[4,10,32,750]{3,1,2,0:T(8,128)(2,1)} copy(bf16[4,10,32,750]{3,2,0,1:T(8,128)(2,1)S(1)} %reshape.20) | data formatting | bytes 3840000 | tf_op jit(solution)/shard_map/reshape | solution.py:34
  46.3 0.0 all-to-all-done.2
  46.3 10.5 %all-to-all-start.1 = ((bf16[128,10,750]{2,1,0:T(8,128)(2,1)}), bf16[128,10,750]{2,1,0:T(8,128)(2,1)S(1)}, u32[]{:S(2)}, u32[]{:S(2)}) async-start(bf16[128,10,750]{2,1,0:T(8,128)(2,1)} %bitcast.22), calls=%async_computation.1 | async-start | bytes 6291456 | tf_op jit(solution)/shard_map/all_to_all | solution.py:44
  56.9 40.6 %all-to-all-done.1 = bf16[128,10,750]{2,1,0:T(8,128)(2,1)S(1)} async-done(((bf16[128,10,750]{2,1,0:T(8,128)(2,1)}), bf16[128,10,750]{2,1,0:T(8,128)(2,1)S(1)}, u32[]{:S(2)}, u32[]{:S(2)}) %all-to-all-start.1) | async-done | bytes 1920032 | tf_op jit(solution)/shard_map/all_to_all | solution.py:44
  97.4 1.8 %stack.3 = bf16[32,40,1024]{2,1,0:T(8,128)(2,1)} broadcast(bf16[40,1024]{1,0:T(8,128)(2,1)S(1)} %stack_reshape.2), dimensions={1,2} | broadcast | bytes 2703360 | tf_op jit(solution)/shard_map/stack | solution.py:11
  99.2 4.8 %all-to-all-start.3 = ((bf16[32,40,1024]{2,1,0:T(8,128)(2,1)}), bf16[32,40,1024]{2,1,0:T(8,128)(2,1)}, u32[]{:S(2)}, u32[]{:S(2)}) async-start(bf16[32,40,1024]{2,1,0:T(8,128)(2,1)} %stack.3), calls=%async_computation.3 | async-start | bytes 5242880 | tf_op jit(solution)/shard_map/all_to_all | solution.py:12
  104.0 2.1 %copy.12 = bf16[32,4,10,750]{3,2,1,0:T(8,128)(2,1)} copy(bf16[32,4,10,750]{3,2,0,1:T(8,128)(2,1)S(1)} %bitcast.21) | data formatting | bytes 3840000 | tf_op jit(solution)/shard_map/transpose | solution.py:18
  106.1 3.9 %reshape_reshape.7 = bf16[1280,750]{1,0:T(8,128)(2,1)S(1)} reshape(bf16[32,4,10,750]{3,2,1,0:T(8,128)(2,1)} %copy.12) | data formatting | bytes 3840000 | tf_op jit(solution)/shard_map/reshape;reshape | solution.py:18
  110.1 30.8 %all-to-all-done.3 = bf16[32,40,1024]{2,1,0:T(8,128)(2,1)} async-done(((bf16[32,40,1024]{2,1,0:T(8,128)(2,1)}), bf16[32,40,1024]{2,1,0:T(8,128)(2,1)}, u32[]{:S(2)}, u32[]{:S(2)}) %all-to-all-start.3) | async-done | bytes 2621472 | tf_op jit(solution)/shard_map/all_to_all | solution.py:12
  140.9 5.6 %fusion.3 = f32[750,1024]{1,0:T(8,128)} fusion(bf16[1280,750]{1,0:T(8,128)(2,1)S(1)} %reshape_reshape.7, bf16[1280,1024]{1,0:T(8,128)(2,1)} %bitcast.8), kind=kOutput, calls=%fused_computation.5 | convolution fusion | flops 1966080000 | bytes 7613440 | tf_op jit(solution)/shard_map/dot_general | solution.py:60
  (1 shorter events, 0.0 us)
Async XLA Ops:
  11.3 35.0 %all-to-all-start.2 = ((bf16[4,10,1024]{2,1,0:T(8,128)(2,1)}), bf16[4,10,1024]{2,1,0:T(8,128)(2,1)S(1)}, u32[]{:S(2)}, u32[]{:S(2)}) async-start(bf16[4,10,1024]{2,1,0:T(8,128)(2,1)} %broadcast_in_dim.5), calls=%async_computation.2 | async-start | bytes 262144 | tf_op jit(solution)/shard_map/all_to_all | solution.py:23
  17.8 12.5 %copy-start = (bf16[10,100,100]{2,1,0:T(8,128)(2,1)S(1)}, bf16[10,100,100]{2,1,0:T(8,128)(2,1)}, u32[]{:S(2)}) copy-start(bf16[10,100,100]{2,1,0:T(8,128)(2,1)} %param.5) | copy-start | bytes 600004
  46.3 51.1 %all-to-all-start.1 = ((bf16[128,10,750]{2,1,0:T(8,128)(2,1)}), bf16[128,10,750]{2,1,0:T(8,128)(2,1)S(1)}, u32[]{:S(2)}, u32[]{:S(2)}) async-start(bf16[128,10,750]{2,1,0:T(8,128)(2,1)} %bitcast.22), calls=%async_computation.1 | async-start | bytes 6291456 | tf_op jit(solution)/shard_map/all_to_all | solution.py:44
  99.2 41.6 %all-to-all-start.3 = ((bf16[32,40,1024]{2,1,0:T(8,128)(2,1)}), bf16[32,40,1024]{2,1,0:T(8,128)(2,1)}, u32[]{:S(2)}, u32[]{:S(2)}) async-start(bf16[32,40,1024]{2,1,0:T(8,128)(2,1)} %stack.3), calls=%async_computation.3 | async-start | bytes 5242880 | tf_op jit(solution)/shard_map/all_to_all | solution.py:12
